TPU v7x, 128 devices: a whole 4x4x4 slice. The times are simulated.
128 devices in a mesh: seq: 32 (over z_hi, y, x), head: 4 (over z_lo, core).
Axes of the slice: x: 4, y: 4, z: 4 (z_hi: 2, z_lo: 2; z = z_hi * 2 + z_lo), core: 2. Of those that a mesh axis runs over, the one named last changes fastest.
Arguments:
- x_in: bfloat16 [16384, 4096], P('seq', 'head'), may hold values from -6 to 6
- z_in: bfloat16 [16384, 4096], P('seq', 'head'), may hold values from -6 to 6
- b_in: bfloat16 [16384, 512], P('seq', 'head'), may hold values from -0.5 to 0.5
- c_in: bfloat16 [16384, 512], P('seq', 'head'), may hold values from -0.5 to 0.5
- dt_raw: float32 [64, 16384], P('head', 'seq')
- dt_bias: float32 [64], P('head'), may hold values from -5 to -4
- a_log: float32 [64], P('head')
- d_skip: float32 [64], P('head'), may hold values from 0.1 to 1.9
- gain: float32 [4096], P('head'), may hold values from 0.5 to 1.5
- resets: int32 [64, 128], P('head', 'seq'), may hold values 0 or 1
- out_weight: bfloat16 [4096, 4096], P('seq', 'head'), may hold values from -0.09375 to 0.09375
- cotangent: bfloat16 [16384, 4096], P('seq', 'head'), may hold values from -6 to 6
Outputs:
- d_x: bfloat16 [16384, 4096], P('seq', 'head')
- d_z: bfloat16 [16384, 4096], P('seq', 'head')
- d_b: bfloat16 [16384, 512], P('seq', 'head')
- d_c: bfloat16 [16384, 512], P('seq', 'head')
- raw_timestep_gradient: float32 [64, 16384], P('head', 'seq')
- d_out_weight: float32 [4096, 4096], P('seq', 'head')
All inputs are finite; a program needn't handle non-finite values. No bound on the sum of `resets` on one device may be relied on, other than what follows from the above.
Results may differ from a plain program's by a relative error of at most 0.0075.
Values may be sent and summed in bfloat16 or wider, within the bound.
A program may use at most 256 MiB of HBM per device.

v0:
```python
from functools import partial

import jax
import jax.numpy as jnp
from jax import lax
from jax.sharding import PartitionSpec as P

HEADDIM = 64
STATE = 128
BLOCK = 128


highest = lax.Precision.HIGHEST


def prefix(value, axis, join, neutral, backward):
    count, mine = (lax.axis_size(axis), lax.axis_index(axis))
    pieces = jax.tree.map(lambda part: lax.all_gather(part, axis), value)
    if backward:
        pieces = jax.tree.map(lambda part: part[::-1], pieces)
        mine = count - 1 - mine
    so_far = jax.tree.map(
        lambda part, zero: jnp.full_like(part, 0) + jnp.asarray(zero, part.dtype), value, neutral
    )

    def step(position, so_far):
        longer = join(so_far, jax.tree.map(lambda part: part[position], pieces))
        return jax.tree.map(lambda new, old: jnp.where(position < mine, new, old), longer, so_far)

    return lax.fori_loop(0, count - 1, step, so_far)


def block_step(state, inputs, per_group, skip_gain):
    x_block, b_block, c_block, rate_block, step_block, keep_block = inputs
    running = jnp.cumsum(rate_block, axis=1)
    positions = rate_block.shape[1]
    lower = jnp.arange(positions)[:, None] >= jnp.arange(positions)[None, :]
    spread = jnp.where(lower[None], running[:, :, None] - running[:, None, :], 0.0)
    decays = jnp.exp(spread) * lower[None].astype(jnp.float32)
    scores = jnp.einsum("tgn,sgn->gts", c_block, b_block, precision=highest)
    scores = jnp.repeat(scores, per_group, axis=0)
    mixing = scores * decays * step_block[:, None, :]
    within = jnp.einsum("hts,shp->thp", mixing, x_block, precision=highest)
    c_heads = jnp.repeat(c_block, per_group, axis=1)
    b_heads = jnp.repeat(b_block, per_group, axis=1)
    carried = state * keep_block[:, None, None]
    incoming = (
        jnp.einsum("thn,hpn->thp", c_heads, carried, precision=highest)
        * jnp.exp(running).T[:, :, None]
    )
    output = within + incoming + skip_gain[None, :, None] * x_block
    weighted = (jnp.exp(running[:, -1:] - running) * step_block).T
    fresh = jnp.einsum("sh,shp,shn->hpn", weighted, x_block, b_heads, precision=highest)
    return (carried * jnp.exp(running[:, -1])[:, None, None] + fresh, output)


def scan_blocks(inputs, bmatrix, cmatrix, dt_raw, start, dt_bias, a_log, d_skip, keep):
    positions = inputs.shape[0]
    heads = dt_raw.shape[0]
    groups = bmatrix.shape[1] // STATE
    blocks = positions // BLOCK
    step_size = jax.nn.softplus(dt_raw + dt_bias[:, None])
    rate = -step_size * jnp.exp(a_log)[:, None]
    x_blocks = inputs.reshape(blocks, BLOCK, heads, HEADDIM)
    b_blocks = bmatrix.reshape(blocks, BLOCK, groups, STATE)
    c_blocks = cmatrix.reshape(blocks, BLOCK, groups, STATE)
    rate_blocks = rate.reshape(heads, blocks, BLOCK).transpose(1, 0, 2)
    step_blocks = step_size.reshape(heads, blocks, BLOCK).transpose(1, 0, 2)
    stepper = partial(block_step, per_group=heads // groups, skip_gain=d_skip)
    final, outputs = lax.scan(
        stepper, start, (x_blocks, b_blocks, c_blocks, rate_blocks, step_blocks, keep.T)
    )
    return (outputs.reshape(positions, heads * HEADDIM), final)


def gate_norm(mixed, gates, gain, groups):
    gated = mixed * jax.nn.silu(gates)
    count = gated.shape[0]
    grouped = gated.reshape(count, groups, -1)
    factor = lax.rsqrt(jnp.mean(grouped * grouped, axis=2, keepdims=True) + 1e-05)
    return (grouped * factor).reshape(count, -1) * gain


def compose(earlier, later):
    return (earlier[0] * later[0], later[0][:, None, None] * earlier[1] + later[1])


def body(
    x_in, z_in, b_in, c_in, dt_raw, dt_bias, a_log, d_skip, gain, resets, out_weight, cotangent
):
    heads = dt_raw.shape[0]
    groups = b_in.shape[1] // STATE
    per_group = heads // groups
    positions = x_in.shape[0]
    keep = 1.0 - resets.astype(jnp.float32)
    x_wide = x_in.astype(jnp.float32)
    input_matrix_wide = b_in.astype(jnp.float32)
    c_wide = c_in.astype(jnp.float32)
    z_wide = z_in.astype(jnp.float32)
    zero_state = jnp.zeros((heads, HEADDIM, STATE), jnp.float32)
    step_size = jax.nn.softplus(dt_raw + dt_bias[:, None])
    rate = -step_size * jnp.exp(a_log)[:, None]
    running = jnp.cumsum(rate, axis=1)
    suffix_rates = jnp.flip(jnp.cumsum(jnp.flip(rate, axis=1), axis=1), axis=1)
    after_rates = jnp.concatenate([suffix_rates[:, 1:], jnp.zeros((heads, 1), jnp.float32)], axis=1)
    keep_upto = jnp.repeat(jnp.cumprod(keep, axis=1), BLOCK, axis=1)
    keep_suffix = jnp.flip(jnp.cumprod(jnp.flip(keep, axis=1), axis=1), axis=1)
    keep_after = jnp.concatenate([keep_suffix[:, 1:], jnp.ones((heads, 1), jnp.float32)], axis=1)
    keep_after = jnp.repeat(keep_after, BLOCK, axis=1)
    to_end = jnp.exp(after_rates) * keep_after * step_size
    x_heads = x_wide.reshape(positions, groups, per_group, HEADDIM)
    b_groups = input_matrix_wide.reshape(positions, groups, STATE)
    c_groups = c_wide.reshape(positions, groups, STATE)
    end_weights = to_end.T.reshape(positions, groups, per_group)
    local_final = jnp.einsum(
        "tgq,tgqp,tgn->gqpn", end_weights, x_heads, b_groups, precision=highest
    ).reshape(heads, HEADDIM, STATE)
    slab_decay = jnp.exp(running[:, -1]) * jnp.prod(keep, axis=1)
    identity = (jnp.ones((heads,), jnp.float32), zero_state)
    entering = prefix((slab_decay, local_final), "seq", compose, identity, False)[1]

    def mixer(x_value, b_value, c_value, raw_steps, start_state):
        return scan_blocks(
            x_value, b_value, c_value, raw_steps, start_state, dt_bias, a_log, d_skip, keep
        )

    (mixed, leaving), mixer_pull = jax.vjp(
        mixer, x_wide, input_matrix_wide, c_wide, dt_raw, entering
    )

    def norming(mixed_value, z_value):
        return gate_norm(mixed_value, z_value, gain, groups)

    normed, norm_pull = jax.vjp(norming, mixed, z_wide)
    normed_half = normed.astype(jnp.bfloat16)
    gathered = lax.all_gather(cotangent, "head", axis=1, tiled=True)
    columns = gathered
    d_normed = jnp.dot(
        columns,
        lax.all_gather(out_weight, "seq", axis=0, tiled=True),
        preferred_element_type=jnp.float32,
    )
    d_mixed, grad_z = norm_pull(d_normed)
    from_start = (jnp.exp(running) * keep_upto).T.reshape(positions, groups, per_group)
    d_heads = d_mixed.reshape(positions, groups, per_group, HEADDIM)
    start_grad = jnp.einsum(
        "tgq,tgqp,tgn->gqpn", from_start, d_heads, c_groups, precision=highest
    ).reshape(heads, HEADDIM, STATE)
    arriving = prefix((slab_decay, start_grad), "seq", compose, identity, True)[1]
    grad_x, grad_b, grad_c, grad_steps, unused = mixer_pull((d_mixed, arriving))
    columns = gathered
    d_out_weight = lax.psum_scatter(
        jnp.einsum("td,ti->di", columns, normed_half, preferred_element_type=jnp.float32),
        "seq",
        scatter_dimension=0,
        tiled=True,
    )
    return (
        grad_x.astype(jnp.bfloat16),
        grad_z.astype(jnp.bfloat16),
        grad_b.astype(jnp.bfloat16),
        grad_c.astype(jnp.bfloat16),
        grad_steps,
        d_out_weight,
    )


def solution(mesh):
    return jax.shard_map(
        body,
        mesh=mesh,
        in_specs=(
            P("seq", "head"),
            P("seq", "head"),
            P("seq", "head"),
            P("seq", "head"),
            P("head", "seq"),
            P("head"),
            P("head"),
            P("head"),
            P("head"),
            P("head", "seq"),
            P("seq", "head"),
            P("seq", "head"),
        ),
        out_specs=(
            P("seq", "head"),
            P("seq", "head"),
            P("seq", "head"),
            P("seq", "head"),
            P("head", "seq"),
            P("seq", "head"),
        ),
        check_vma=False,
    )
```

profile of v0, /device:TPU:0, one launch (start us, length us, event | category | flops | bytes accessed | tf_op | source)
XLA Modules:
  0.0 737.6 jit_solution(9167421800133413308)
XLA Ops:
  21.2 96.9 %all-gather.2 = f32[32,1,16]{2,1,0:T(1,128)S(1)} all-gather(f32[1,1,16]{2,1,0:T(1,128)S(1)} %fusion.127), channel_id=1, replica_groups=mesh['seq'=32,'head'=4] {'seq'}, dimensions={0}, use_global_device_ids=true | all-gather | bytes 2112 | tf_op jit(solution)/shard_map/all_gather | solution.py:18
  121.8 53.0 %all-gather.12.cloned.1.call-done = f32[512,64,128]{2,1,0:T(8,128)} async-done(((f32[16,64,128]{2,1,0:T(8,128)}), f32[512,64,128]{2,1,0:T(8,128)}) %all-gather.12.cloned.1.call-update) | async-done | bytes 16777232 | tf_op jit(solution)/shard_map/all_gather | solution.py:18
  174.8 37.9 %while.110 = (s32[]{:T(128)}, f32[16,64,128]{2,1,0:T(8,128)S(1)}, s32[]{:T(128)}, f32[32,16]{1,0:T(8,128)S(1)}, f32[32,16,64,128]{3,2,1,0:T(8,128)}) while((s32[]{:T(128)}, f32[16,64,128]{2,1,0:T(8,128)S(1)}, s32[]{:T(128)}, f32[32,16]{1,0:T(8,128)S(1)}, f32[32,16,64,128]{3,2,1,0:T(8,128)}) %tuple.254), condition=%wide.region_8.9_spmd.clone.clone, body=%wide.region_7.8_spmd.clone.sunk.clone | while | flops 524292 | bytes 1573145 | solution.py:30
  215.4 83.1 %while.109 = (s32[]{:T(128)}, f32[16,64,128]{2,1,0:T(8,128)S(1)}, f32[4,128,16,64]{1,3,2,0:T(8,128)}, f32[4,16,128,128]{3,2,1,0:T(8,128)}, f32[4,16,128,128]{3,2...) while((s32[]{:T(128)}, f32[16,64,128]{2,1,0:T(8,128)S(1)}, ...), condition=%wide.region_11.12_spmd.clone.clone.clone, body=%wide.region_9.11_spmd.clone.clone.sunk.clone | while | flops 633511936 | bytes 16000793 | solution.py:70
  218.6 2.9 multiply_dynamic-update-slice_fusion.3
  221.5 3.0 bitcast_dynamic-update-slice_fusion.23
  224.5 3.7 fusion.254
  239.4 2.9 multiply_dynamic-update-slice_fusion.3
  242.4 3.0 bitcast_dynamic-update-slice_fusion.23
  245.3 3.7 fusion.254
  260.2 2.9 multiply_dynamic-update-slice_fusion.3
  263.1 2.9 bitcast_dynamic-update-slice_fusion.23
  266.1 3.7 fusion.254
  280.7 3.1 multiply_dynamic-update-slice_fusion.3
  283.9 3.0 bitcast_dynamic-update-slice_fusion.23
  286.9 3.7 fusion.254
  298.5 4.7 copy.179
  303.3 4.8 reshape.531
  308.1 21.0 %all-gather.10.cloned.1.call-done = bf16[4096,1024]{1,0:T(8,128)(2,1)} async-done(((bf16[128,1024]{1,0:T(8,128)(2,1)}), bf16[4096,1024]{1,0:T(8,128)(2,1)}) %all-gather.10.cloned.1.call-update) | async-done | bytes 8388624 | tf_op jit(solution)/shard_map/all_gather | solution.py:140
  329.2 10.6 %multiply_reduce_fusion.1 = (f32[512]{0:T(512)S(1)}, f32[512]{0:T(512)S(1)}, f32[512,1024]{1,0:T(8,128)S(1)}) fusion(f32[512,1024]{1,0:T(8,128)} %reshape.531, bf16[512,1024]{1,0:T(8,128)(2,1)} %param.21, f32[1024]{0:T(1024)S(1)} %copy-done.15, bf16[512,4096]{1,0:T(8,128)(2,1)} %all-gather.8.cloned.1.call-done, ...), kind=kOutput, calls=%fused_computation.184 | convolution fusion | flops 4300733440 | bytes 17833984 | tf_op jit(solution)/shard_map/dot_general | solution.py:138
  339.8 3.6 fusion.104
  345.3 3.5 fusion.105
  348.9 13.9 %convolution_bitcast_fusion.4 = f32[4096,1024]{0,1:T(8,128)} fusion(bf16[512,4096]{1,0:T(8,128)(2,1)} %all-gather.8.cloned.1.call-done, f32[512]{0:T(512)S(1)} %get-tuple-element.1859, f32[1024]{0:T(1024)S(1)} %copy-done.15, f32[512,1024]{1,0:T(8,128)} %reshape.531, bf16[512,1024]{1,0:T(8,128)(2,1)} %param.21), kind=kOutput, calls=%fused_computation.168 | convolution fusion | flops 4299685888 | bytes 24123392 | tf_op jit(solution)/shard_map/td,ti->di/dot_general | solution.py:153
  364.9 2.6 reshape.529
  367.5 3.1 copy.152
  370.6 132.0 %all-gather.14.cloned.1.call-done = f32[512,64,128]{2,1,0:T(8,128)} async-done(((f32[16,64,128]{2,1,0:T(8,128)}), f32[512,64,128]{2,1,0:T(8,128)}) %all-gather.14.cloned.1.call-update) | async-done | bytes 16777232 | tf_op jit(solution)/shard_map/all_gather | solution.py:18
  502.6 11.8 %rev.19 = f32[32,16,64,128]{3,2,1,0:T(8,128)} reverse(f32[32,16,64,128]{3,2,1,0:T(8,128)} %bitcast.594), dimensions={0} | reverse | bytes 33554432 | tf_op jit(solution)/shard_map/rev | solution.py:20
  514.4 37.8 %while.111 = (s32[]{:T(128)}, f32[16,64,128]{2,1,0:T(8,128)S(1)}, s32[]{:T(128)}, f32[32,16]{1,0:T(8,128)S(1)}, f32[32,16,64,128]{3,2,1,0:T(8,128)}) while((s32[]{:T(128)}, f32[16,64,128]{2,1,0:T(8,128)S(1)}, s32[]{:T(128)}, f32[32,16]{1,0:T(8,128)S(1)}, f32[32,16,64,128]{3,2,1,0:T(8,128)}) %tuple.234), condition=%wide.region_15.16_spmd.clone.clone, body=%wide.region_14.15_spmd.clone.sunk.clone | while | flops 524292 | bytes 1573145 | solution.py:30
  554.9 163.1 %while.108 = (s32[]{:T(128)}, f32[16,64,128]{2,1,0:T(8,128)S(1)}, bf16[4,128,16,64]{1,3,2,0:T(8,128)(2,1)}, bf16[4,128,1,128]{3,1,2,0:T(8,128)(2,1)}, bf16[4,128...) while((s32[]{:T(128)}, f32[16,64,128]{2,1,0:T(8,128)S(1)}, ...), condition=%wide.region_25.26_spmd.clone.clone, body=%wide.region_16.25_spmd.clone.sunk.clone | while | flops 1263466496 | bytes 32037560 | solution.py:70
  555.1 2.7 constant_dynamic-slice_fusion.16
  557.8 3.3 fusion.236
  565.4 5.0 fusion.238
  583.7 3.1 fusion.237
  595.8 2.7 constant_dynamic-slice_fusion.16
  598.5 3.3 fusion.236
  606.1 5.0 fusion.238
  624.4 3.1 fusion.237
  636.5 2.7 constant_dynamic-slice_fusion.16
  639.2 3.3 fusion.236
  646.8 5.0 fusion.238
  665.1 3.1 fusion.237
  677.2 2.7 constant_dynamic-slice_fusion.16
  679.9 3.3 fusion.236
  687.5 5.0 fusion.238
  705.8 3.1 fusion.237
  719.0 2.7 copy.177
  721.7 2.3 reshape.530
  724.7 4.1 reduce-scatter.2.cloned.1.call-done
  (471 shorter events, 255.4 us)
Async XLA Ops:
  7.2 167.6 %all-gather.12.cloned.1.call-start = ((), (), s32[]{:S(2)}) async-start(), calls=%async_computation.4 | async-start | bytes 17301504 | tf_op jit(solution)/shard_map/all_gather | solution.py:18
  7.9 0.9 copy-start.16
  13.3 0.8 copy-start.5
  13.3 0.8 copy-start.13
  13.3 0.9 copy-start.3
  14.2 3.5 copy-start.12
  16.2 292.0 %all-gather.8.cloned.1.call-start = ((), (), s32[]{:S(2)}) async-start(), calls=%async_computation.1 | async-start | bytes 5242880 | tf_op jit(solution)/shard_map/all_gather | solution.py:136
  16.9 312.3 %all-gather.10.cloned.1.call-start = ((), (), s32[]{:S(2)}) async-start(), calls=%async_computation.2 | async-start | bytes 8650752 | tf_op jit(solution)/shard_map/all_gather | solution.py:140
  17.6 485.0 %all-gather.14.cloned.1.call-start = ((), (), s32[]{:S(2)}) async-start(), calls=%async_computation.5 | async-start | bytes 17301504 | tf_op jit(solution)/shard_map/all_gather | solution.py:18
  118.1 1.9 copy-start.4
  298.5 4.8 copy-start.1
  303.3 25.9 %copy-start.15 = (f32[1024]{0:T(1024)S(1)}, f32[1024]{0:T(1024)}, u32[]{:S(2)}) copy-start(f32[1024]{0:T(1024)} %param.28) | copy-start | bytes 12292
  329.2 10.6 %copy-start.2 = (f32[512,1024]{1,0:T(8,128)S(1)}, f32[512,1024]{1,0:T(8,128)}, u32[]{:S(2)}) copy-start(f32[512,1024]{1,0:T(8,128)} %reshape.531) | copy-start | bytes 6291460
  348.8 380.0 %reduce-scatter.2.cloned.1.call-start = ((), (), s32[]{:S(2)}) async-start(), calls=%async_computation.3 | async-start | bytes 17301504 | tf_op jit(solution)/shard_map/reduce_scatter | solution.py:152
  583.7 6.6 copy-start
  588.8 5.8 copy-start.9
  590.3 4.6 copy-start.7
  594.9 0.7 copy-start.10
  595.2 0.7 copy-start.8
  624.4 6.5 copy-start
  629.6 5.7 copy-start.9
  630.9 4.6 copy-start.7
  635.5 0.7 copy-start.10
  635.9 0.7 copy-start.8
  665.1 6.5 copy-start
  670.3 5.7 copy-start.9
  671.6 4.6 copy-start.7
  676.2 0.7 copy-start.10
  676.6 0.7 copy-start.8
  705.8 6.6 copy-start
  710.9 5.8 copy-start.9
  712.4 4.6 copy-start.7
  717.0 0.7 copy-start.10
  717.3 0.7 copy-start.8
  721.6 2.3 copy-start.6
  721.7 2.3 copy-start.11
  721.7 2.3 copy-start.14
  721.7 2.3 copy-start.17
Sparse Core Ops, SparseCore 0:
  16.3 158.4 all-gather.11
  176.4 43.5 all-gather.7
  223.1 106.0 all-gather.9
  348.9 153.6 all-gather.13
  504.9 223.9 reduce-scatter.1
where the time goes:
time: 748 us; the launch traced here: 738 us
  waiting for transfers between devices  212 us (28%)
  other arithmetic  151 us (20%)
  local copies, waits for them, and re-layouts  131 us (18%)
  matrix products  131 us (18%)
  blocking collectives  96.9 us (13%)
  between operations  14.4 us (2%)
    all_gather x2, waiting for transfers between devices, prefix(): pieces = jax.tree.map(lambda part: lax.all_gather(part, axis), value)  185 us
    all_gather x1, blocking collectives, prefix(): pieces = jax.tree.map(lambda part: lax.all_gather(part, axis), value)  96.9 us
    select_n x62, other arithmetic, step(): jnp.where(position < mine, new, old)  73.1 us
    dot_general x12, matrix products, block_step(): within = jnp.einsum('hts,shp->thp', mixing, x_block, precision=highest)  47 us
    dynamic_update_slice x24, other arithmetic, scan_blocks(): lax.scan(stepper, start, (x_blocks, b_blocks, c_blocks, rate_blocks, step...  26.9 us
    dynamic_slice x20, local copies, waits for them, and re-layouts, scan_blocks(): lax.scan(stepper, start, (x_blocks, b_blocks, c_blocks, rate_blocks, step...  25.6 us
    dot_general x12, matrix products, block_step(): jnp.einsum('thn,hpn->thp', c_heads, carried, precision=highest)  25.6 us
    dot_general x12, matrix products, block_step(): jnp.einsum('sh,shp,shn->hpn', weighted, x_block, b_heads, precision=highest)  25.3 us
  transfers between devices with their start and end apart: 5, of which 4 were waited for; matrix products, arithmetic and copies ran while one was open for 51% of the time, Pallas kernels for 0%

commit v1 on v0

v1 whole, which is shorter than its diff:
```python
import jax
import jax.numpy as jnp
from jax import lax
from jax.sharding import PartitionSpec as P

HEADDIM = 64
STATE = 128
BLOCK = 128


high = lax.Precision.HIGH
highest = lax.Precision.HIGHEST


def gate_norm(mixed, gates, gain, groups):
    gated = mixed * jax.nn.silu(gates)
    count = gated.shape[0]
    grouped = gated.reshape(count, groups, -1)
    factor = lax.rsqrt(jnp.mean(grouped * grouped, axis=2, keepdims=True) + 1e-05)
    return (grouped * factor).reshape(count, -1) * gain


def exchange(value):
    return lax.all_to_all(value, "seq", split_axis=1, concat_axis=0, tiled=False)


def give_back(value, shape):
    parts = lax.all_to_all(value, "seq", split_axis=0, concat_axis=1, tiled=False)
    return parts.reshape(shape)


def local_terms(x_value, b_value, c_value, raw_steps, dt_bias, a_log, d_skip):
    heads = raw_steps.shape[0]
    blocks = x_value.shape[0]
    step_size = jax.nn.softplus(raw_steps + dt_bias[:, None])
    rate = -step_size * jnp.exp(a_log)[:, None]
    rate = rate.reshape(heads, blocks, BLOCK)
    step_size = step_size.reshape(heads, blocks, BLOCK)
    running = jnp.cumsum(rate, axis=2)
    lower = jnp.arange(BLOCK)[:, None] >= jnp.arange(BLOCK)[None, :]
    spread = jnp.where(lower, running[:, :, :, None] - running[:, :, None, :], 0.0)
    decays = jnp.exp(spread) * lower.astype(jnp.float32)
    scores = jnp.einsum("ktn,ksn->kts", c_value, b_value, precision=high)
    mixing = scores[None] * decays * step_size[:, :, None, :]
    within = jnp.einsum("hkts,kshp->kthp", mixing, x_value, precision=high)
    local = within + d_skip[:, None] * x_value
    weighted = jnp.exp(running[:, :, -1:] - running) * step_size
    scaled = x_value * weighted.transpose(1, 2, 0)[:, :, :, None]
    fresh = jnp.einsum("kshp,ksn->khpn", scaled, b_value, precision=high)
    block_decay = jnp.exp(running[:, :, -1])
    from_start = jnp.exp(running).transpose(1, 2, 0)
    return local, fresh, block_decay, from_start


def chain(fresh, block_decay, keep, start):
    state = start
    entering = []
    for block in range(fresh.shape[0]):
        carried = state * keep[:, block, None, None]
        entering.append(carried)
        state = carried * block_decay[:, block, None, None] + fresh[block]
    return jnp.stack(entering), state


def from_states(c_value, carried, from_start):
    incoming = jnp.einsum("ktn,khpn->kthp", c_value, carried, precision=high)
    return incoming * from_start[:, :, :, None]


def body(
    x_in, z_in, b_in, c_in, dt_raw, dt_bias, a_log, d_skip, gain, resets, out_weight, cotangent
):
    heads = dt_raw.shape[0]
    groups = b_in.shape[1] // STATE
    positions = x_in.shape[0]
    blocks = positions // BLOCK
    count = lax.axis_size("seq")
    share = HEADDIM // count
    shape = (heads, HEADDIM, STATE)
    weight = lax.all_gather(out_weight, "seq", axis=0, tiled=True)
    gathered = lax.all_gather(cotangent, "head", axis=0, tiled=False)
    keep = 1.0 - resets.astype(jnp.float32)
    x_wide = x_in.astype(jnp.float32).reshape(blocks, BLOCK, heads, HEADDIM)
    b_wide = b_in.astype(jnp.float32).reshape(blocks, BLOCK, STATE)
    c_wide = c_in.astype(jnp.float32).reshape(blocks, BLOCK, STATE)
    z_wide = z_in.astype(jnp.float32)

    def local_part(x_value, b_value, c_value, raw_steps):
        return local_terms(x_value, b_value, c_value, raw_steps, dt_bias, a_log, d_skip)

    (local, fresh, block_decay, from_start), local_pull = jax.vjp(
        local_part, x_wide, b_wide, c_wide, dt_raw
    )
    own = chain(fresh, block_decay, keep, jnp.zeros(shape, jnp.float32))[1]
    slab_decay = jnp.prod(block_decay * keep, axis=1)
    marks = jnp.broadcast_to(slab_decay[:, None, None, None], (heads, count, 1, STATE))
    outgoing = jnp.concatenate([own.reshape(heads, count, share, STATE), marks], axis=2)
    pieces = exchange(outgoing)
    slab_decays = pieces[:, :, share, 0]
    place = jnp.arange(count)
    between = (place[None, None, :] < place[:, None, None]) & (
        place[None, None, :] > place[None, :, None]
    )
    factors = jnp.where(between[None], slab_decays.T[:, None, None, :], 1.0)
    earlier = (place[None, :] < place[:, None]).astype(jnp.float32)
    paths = jnp.prod(factors, axis=3) * earlier[None]
    summed = jnp.einsum("hji,ihpn->jhpn", paths, pieces[:, :, :share], precision=highest)
    entering = give_back(summed, shape)

    def states(fresh_value, decay_value, start):
        return chain(fresh_value, decay_value, keep, start)

    (carried, leaving), states_pull = jax.vjp(states, fresh, block_decay, entering)
    incoming, incoming_pull = jax.vjp(from_states, c_wide, carried, from_start)
    mixed = (local + incoming).reshape(positions, heads * HEADDIM)

    def norming(mixed_value, z_value):
        return gate_norm(mixed_value, z_value, gain, groups)

    normed, norm_pull = jax.vjp(norming, mixed, z_wide)
    normed_half = normed.astype(jnp.bfloat16)
    owners = gathered.shape[0]
    d_out_weight = lax.psum_scatter(
        jnp.einsum("gtd,ti->gdi", gathered, normed_half, preferred_element_type=jnp.float32)
        .reshape(out_weight.shape[0] * count, normed_half.shape[1]),
        "seq",
        scatter_dimension=0,
        tiled=True,
    )
    d_normed = jnp.einsum(
        "gtd,gdi->ti",
        gathered,
        weight.reshape(owners, -1, weight.shape[1]),
        preferred_element_type=jnp.float32,
    )
    d_mixed, grad_z = norm_pull(d_normed)
    d_local = d_mixed.reshape(blocks, BLOCK, heads, HEADDIM)
    grad_c_states, d_carried, d_from_start = incoming_pull(d_local)
    start_grad = states_pull((d_carried, jnp.zeros(shape, jnp.float32)))[2]
    back_pieces = exchange(start_grad.reshape(heads, count, share, STATE))
    back_summed = jnp.einsum("hij,ihpn->jhpn", paths, back_pieces, precision=highest)
    arriving = give_back(back_summed, shape)
    d_fresh, d_block_decay, unused = states_pull((d_carried, arriving))
    grad_x, grad_b, grad_c, grad_steps = local_pull(
        (d_local, d_fresh, d_block_decay, d_from_start)
    )
    grad_c = grad_c + grad_c_states
    return (
        grad_x.reshape(positions, heads * HEADDIM).astype(jnp.bfloat16),
        grad_z.astype(jnp.bfloat16),
        grad_b.reshape(positions, STATE).astype(jnp.bfloat16),
        grad_c.reshape(positions, STATE).astype(jnp.bfloat16),
        grad_steps,
        d_out_weight,
    )


def solution(mesh):
    return jax.shard_map(
        body,
        mesh=mesh,
        in_specs=(
            P("seq", "head"),
            P("seq", "head"),
            P("seq", "head"),
            P("seq", "head"),
            P("head", "seq"),
            P("head"),
            P("head"),
            P("head"),
            P("head"),
            P("head", "seq"),
            P("seq", "head"),
            P("seq", "head"),
        ),
        out_specs=(
            P("seq", "head"),
            P("seq", "head"),
            P("seq", "head"),
            P("seq", "head"),
            P("head", "seq"),
            P("seq", "head"),
        ),
        check_vma=False,
    )
```

time: 748 us -> 444 us (0.59)
  other arithmetic: 151 us -> 41.3 us
  blocking collectives: 96.9 us -> 0 us
  local copies, waits for them, and re-layouts: 131 us -> 43.6 us
  matrix products: 131 us -> 61.3 us
  waiting for transfers between devices: 212 us -> 249 us
  starting transfers between devices: 0.2 us -> 26.9 us
    all_gather x4 -> x2, waiting for transfers between devices: 206 us -> 75.3 us  [the longest x1 75.3 us: body(): weight = lax.all_gather(out_weight, 'seq', axis=0, tiled=True)]
    reduce_scatter x1, waiting for transfers between devices: 4.12 us -> 128 us  [body(): lax.psum_scatter(jnp.einsum('gtd,ti->gdi', gathered, normed_half, preferr...]
    all_gather x1 -> x0, blocking collectives: 96.9 us -> none  [prefix(): pieces = jax.tree.map(lambda part: lax.all_gather(part, axis), value)]
    select_n x63 -> x0, other arithmetic: 74 us -> none  [the longest x62 73.1 us: step(): jnp.where(position < mine, new, old)]
    dot_general x52 -> x16, matrix products: 131 us -> 61.3 us  [the longest x3 17.7 us: local_terms(): within = jnp.einsum('hkts,kshp->kthp', mixing, x_value, precision=high)]
    all_to_all x0 -> x4, waiting for transfers between devices: none -> 44.9 us  [the longest x2 23.2 us: give_back(): lax.all_to_all(value, 'seq', split_axis=0, concat_axis=1, tiled=False)]
    dynamic_update_slice x24 -> x0, other arithmetic: 26.9 us -> none  [scan_blocks(): lax.scan(stepper, start, (x_blocks, b_blocks, c_blocks, rate_blocks, step...]
    all_to_all x0 -> x4, starting transfers between devices: none -> 26.8 us  [the longest x2 17 us: exchange(): lax.all_to_all(value, 'seq', split_axis=1, concat_axis=0, tiled=False)]
  transfers between devices with their start and end apart: 5 -> 7, of which waited for: 4 -> 6; matrix products, arithmetic and copies ran while one was open for 51% -> 27% of each run, Pallas kernels for 0% -> 0%
where the time goes in v1:
time: 444 us; the launch traced here: 438 us
  waiting for transfers between devices  249 us (56%)
  matrix products  61.3 us (14%)
  local copies, waits for them, and re-layouts  43.6 us (10%)
  other arithmetic  41.3 us (9%)
  starting transfers between devices  26.9 us (6%)
  between operations  15.1 us (3%)
    reduce_scatter x1, waiting for transfers between devices, body(): lax.psum_scatter(jnp.einsum('gtd,ti->gdi', gathered, normed_half, preferr...  128 us
    all_gather x1, waiting for transfers between devices, body(): weight = lax.all_gather(out_weight, 'seq', axis=0, tiled=True)  75.3 us
    all_to_all x2, waiting for transfers between devices, give_back(): lax.all_to_all(value, 'seq', split_axis=0, concat_axis=1, tiled=False)  23.2 us
    all_to_all x2, waiting for transfers between devices, exchange(): lax.all_to_all(value, 'seq', split_axis=1, concat_axis=0, tiled=False)  21.7 us
    dot_general x3, matrix products, local_terms(): within = jnp.einsum('hkts,kshp->kthp', mixing, x_value, precision=high)  17.7 us
    all_to_all x2, starting transfers between devices, exchange(): lax.all_to_all(value, 'seq', split_axis=1, concat_axis=0, tiled=False)  17 us
    dot_general x1, matrix products, body(): jnp.einsum('gtd,gdi->ti', gathered, weight.reshape(owners, -1, weight.sha...  11.8 us
    unnamed x192, local copies, waits for them, and re-layouts  10.6 us
  transfers between devices with their start and end apart: 7, of which 6 were waited for; matrix products, arithmetic and copies ran while one was open for 27% of the time, Pallas kernels for 0%

profile of v1, /device:TPU:0, one launch (start us, length us, event | category | flops | bytes accessed | tf_op | source)
XLA Modules:
  0.0 437.7 jit_solution(16352377933483447845)
XLA Ops:
  9.3 3.0 reshape.340
  12.3 1.8 copy.279
  23.0 11.0 %all-to-all-start = ((f32[1,16,32,3,128]{4,1,3,0,2:T(8,128)}), f32[1,16,32,3,128]{4,1,3,0,2:T(8,128)}, u32[]{:S(2)}, u32[]{:S(2)}) async-start(f32[1,16,32,3,128]{4,1,3,0,2:T(8,128)} %maximum_bitcast_fusion), calls=%async_computation | async-start | bytes 1572864 | tf_op jit(solution)/shard_map/all_to_all | solution.py:24
  34.8 14.7 %all-to-all-done = f32[1,16,32,3,128]{4,1,3,0,2:T(8,128)} async-done(((f32[1,16,32,3,128]{4,1,3,0,2:T(8,128)}), f32[1,16,32,3,128]{4,1,3,0,2:T(8,128)}, u32[]{:S(2)}, u32[]{:S(2)}) %all-to-all-start) | async-done | bytes 786464 | tf_op jit(solution)/shard_map/all_to_all | solution.py:24
  49.4 1.4 copy.541
  51.0 9.6 %select_reduce_fusion = f32[16,32,32]{2,1,0:T(8,128)S(1)} fusion(f32[16,32]{1,0:T(8,128)S(1)} %bitcast.316, pred[32,32,32]{2,1,0:T(8,128)(4,1)} %broadcast_and_fusion), kind=kLoop, calls=%fused_computation | loop fusion | flops 1032192 | bytes 100352 | tf_op jit(solution)/shard_map/reduce_prod | solution.py:106
  60.6 1.9 convolution_bitcast_fusion.1
  62.6 1.2 copy.287
  63.8 4.7 %all-to-all-start.1 = ((f32[32,16,1,2,128]{4,3,1,2,0:T(2,128)}), f32[32,16,1,2,128]{4,3,1,2,0:T(2,128)}, u32[]{:S(2)}, u32[]{:S(2)}) async-start(f32[32,16,1,2,128]{4,3,1,2,0:T(2,128)} %copy.287), calls=%async_computation.1 | async-start | bytes 1048576 | tf_op jit(solution)/shard_map/all_to_all | solution.py:28
  69.2 1.8 fusion.148
  71.0 10.2 %all-to-all-done.1 = f32[32,16,1,2,128]{4,3,1,2,0:T(2,128)} async-done(((f32[32,16,1,2,128]{4,3,1,2,0:T(2,128)}), f32[32,16,1,2,128]{4,3,1,2,0:T(2,128)}, u32[]{:S(2)}, u32[]{:S(2)}) %all-to-all-start.1) | async-done | bytes 524320 | tf_op jit(solution)/shard_map/all_to_all | solution.py:28
  81.2 1.4 copy.543
  85.0 1.3 copy-done.7
  86.4 5.1 %fusion.13 = f32[4,128,16,64]{1,3,2,0:T(8,128)} fusion(bf16[4,128,16,64]{1,3,2,0:T(8,128)(2,1)S(1)} %copy.279, f32[4,16,64,128]{3,2,1,0:T(8,128)S(1)} %fusion.54, f32[16,4,128]{2,0,1:T(8,128)S(1)} %copy-done.50, f32[128,128]{1,0:T(8,128)S(1)} %copy-done.48, f32[16,4,128]{2,0,1:T(8,128)S(1)} %copy-done.35, f32[4,128,128]{2,1,0:T(8,128)S(1)} %copy-done.41, ...), kind=kOutput, calls=%fused_computation.25 | convolution fusion | flops 410517504 | bytes 5685312 | tf_op jit(solution)/shard_map/jvp(hkts,kshp->kthp)/dot_general | solution.py:45
  91.5 4.0 copy.375
  95.5 4.9 %reshape.341 = f32[512,1024]{1,0:T(8,128)} reshape(f32[4,128,16,64]{3,2,1,0:T(8,128)} %copy.375) | data formatting | bytes 4194304 | tf_op jit(solution)/shard_map/reshape | solution.py:115
  100.3 75.3 %all-gather.4.cloned.1.call-done = bf16[4096,1024]{1,0:T(8,128)(2,1)} async-done(((bf16[128,1024]{1,0:T(8,128)(2,1)}), bf16[4096,1024]{1,0:T(8,128)(2,1)}) %all-gather.4.cloned.1.call-update) | async-done | bytes 8388624 | tf_op jit(solution)/shard_map/all_gather | solution.py:80
  175.6 11.8 %multiply_reduce_fusion.2 = (f32[512]{0:T(512)S(1)}, f32[512]{0:T(512)S(1)}, f32[512,1024,1]{1,0,2:T(8,128)}) fusion(f32[512,1024]{1,0:T(8,128)} %reshape.341, bf16[512,1024]{1,0:T(8,128)(2,1)} %param.13, f32[1024]{0:T(1024)} %param.20, bf16[4,512,1024]{2,1,0:T(8,128)(2,1)} %bitcast.323, bf16[4,1024,1024]{2,1,0:T(8,128)(2,1)} %bitcast.322), kind=kOutput, calls=%fused_computation.45 | convolution fusion | flops 4300733440 | bytes 17833984 | tf_op jit(solution)/shard_map/gtd,gdi->ti/dot_general | solution.py:130
  188.0 9.0 %fusion.62 = f32[1024,4,1024]{0,2,1:T(8,128)} fusion(bf16[4,512,1024]{2,1,0:T(8,128)(2,1)S(1)} %bitcast.324, f32[512]{0:T(512)S(1)} %get-tuple-element.78, f32[1024]{0:T(1024)S(1)} %copy-done.85, f32[512,1024]{1,0:T(8,128)S(1)} %copy-done.6, bf16[512,1024]{1,0:T(8,128)(2,1)S(1)} %copy-done.32), kind=kOutput, calls=%fused_computation.80 | convolution fusion | flops 4299685888 | bytes 24123392 | tf_op jit(solution)/shard_map/gtd,ti->gdi/dot_general | solution.py:124
  197.0 4.5 %fusion.20 = (bf16[512,1024]{1,0:T(8,128)(2,1)}, f32[512,1024]{1,0:T(8,128)}) fusion(bf16[512,1024]{1,0:T(8,128)(2,1)} %param.13, f32[512,1024]{1,0:T(8,128)} %reshape.341, f32[512]{0:T(512)} %get-tuple-element.79, f32[512,1024,1]{1,0,2:T(8,128)} %get-tuple-element.91, f32[512]{0:T(512)} %copy-done.84, f32[1024]{0:T(1024)} %param.20), kind=kLoop, calls=%fused_computation.32 | loop fusion | flops 10485760 | bytes 8396800 | tf_op jit(solution)/shard_map/convert_element_type | solution.py:150
  201.5 2.9 copy.293
  204.4 2.9 reshape.325
  207.3 2.3 fusion.43
  212.2 1.2 copy.303
  213.4 6.0 %all-to-all-start.2 = ((f32[1,16,32,2,128]{4,3,1,0,2:T(2,128)}), f32[1,16,32,2,128]{4,3,1,0,2:T(2,128)}, u32[]{:S(2)}, u32[]{:S(2)}) async-start(f32[1,16,32,2,128]{4,3,1,0,2:T(2,128)} %copy.303), calls=%async_computation.2 | async-start | bytes 1048576 | tf_op jit(solution)/shard_map/all_to_all | solution.py:24
  219.5 4.9 %fusion.56 = f32[4,128,128]{2,1,0:T(8,128)} fusion(f32[1,16,64,128]{3,2,1,0:T(8,128)} %copy-done.22, f32[1,16,64,128]{3,2,1,0:T(8,128)} %copy-done.23, f32[1,16,64,128]{3,2,1,0:T(8,128)} %copy-done.24, f32[1,16,64,128]{3,2,1,0:T(8,128)} %copy-done.25, f32[4,128,16,64]{1,0,3,2:T(4,128)} %reshape.325, f32[4,128,16]{1,2,0:T(8,128)} %get-tuple-element.74), kind=kOutput, calls=%fused_computation.76 | convolution fusion | flops 404750336 | bytes 4489216 | tf_op jit(solution)/shard_map/transpose(jvp(ktn,khpn->kthp))/dot_general | solution.py:66
  224.4 6.8 %fusion.11 = (f32[16,4,128]{2,0,1:T(8,128)}, f32[16,4,128]{2,0,1:T(8,128)}, f32[16,4,128]{2,0,1:T(8,128)}, f32[4,128,128]{2,1,0:T(8,128)}) fusion(f32[16,4,128]{2,0,1:T(8,128)S(1)} %copy-done.51, f32[128,128]{1,0:T(8,128)S(1)} %copy-done.49, f32[16,4,128]{2,0,1:T(8,128)S(1)} %copy-done.36, f32[4,128,128]{2,1,0:T(8,128)S(1)} %copy-done.42, ...), kind=kOutput, calls=%fused_computation.23 | convolution fusion | flops 418291712 | bytes 3915776 | tf_op jit(solution)/shard_map/transpose(jvp(hkts,kshp->kthp))/dot_general | solution.py:45
  231.2 7.0 %all-to-all-done.2 = f32[1,16,32,2,128]{4,3,1,0,2:T(2,128)} async-done(((f32[1,16,32,2,128]{4,3,1,0,2:T(2,128)}), f32[1,16,32,2,128]{4,3,1,0,2:T(2,128)}, u32[]{:S(2)}, u32[]{:S(2)}) %all-to-all-start.2) | async-done | bytes 524320 | tf_op jit(solution)/shard_map/all_to_all | solution.py:24
  238.2 2.0 convolution_bitcast_fusion
  240.2 1.2 copy.306
  241.4 5.1 %all-to-all-start.3 = ((f32[32,16,1,2,128]{4,3,1,2,0:T(2,128)}), f32[32,16,1,2,128]{4,3,1,2,0:T(2,128)}, u32[]{:S(2)}, u32[]{:S(2)}) async-start(f32[32,16,1,2,128]{4,3,1,2,0:T(2,128)} %copy.306), calls=%async_computation.3 | async-start | bytes 1048576 | tf_op jit(solution)/shard_map/all_to_all | solution.py:28
  246.5 1.8 fusion.60
  248.4 3.3 fusion.23
  251.7 13.0 %all-to-all-done.3 = f32[32,16,1,2,128]{4,3,1,2,0:T(2,128)} async-done(((f32[32,16,1,2,128]{4,3,1,2,0:T(2,128)}), f32[32,16,1,2,128]{4,3,1,2,0:T(2,128)}, u32[]{:S(2)}, u32[]{:S(2)}) %all-to-all-start.3) | async-done | bytes 524320 | tf_op jit(solution)/shard_map/all_to_all | solution.py:28
  264.7 1.5 copy.542
  266.7 2.4 fusion.87
  269.1 2.5 fusion.91
  272.2 1.3 copy.336
  273.5 1.4 add_multiply_fusion
  275.0 2.3 fusion.14
  278.7 1.6 fusion.130
  280.3 6.3 %reduce_window_sum.23 = f32[16,4,128]{2,0,1:T(8,128)} reduce-window(f32[16,4,128]{2,0,1:T(8,128)} %fusion.130, f32[]{:T(128)} %constant.13.clone.1), window={size=1x1x128 pad=0_0x0_0x0_127}, to_apply=%region_16.17 | reduce-window | flops 1040384 | bytes 65540 | tf_op jit(solution)/shard_map/transpose(jvp(jit(cumsum)))/reduce_window_sum | solution.py:39
  286.5 5.7 %fusion.21 = bf16[4,128,16,64]{1,3,2,0:T(8,128)(2,1)} fusion(f32[4,16,64,128]{3,2,1,0:T(8,128)} %get-tuple-element.93, f32[4,128,16,64]{1,0,3,2:T(4,128)S(1)} %copy-done.5, f32[16,4,128]{2,0,1:T(8,128)} %get-tuple-element.94, f32[128,128]{1,0:T(8,128)} %get-tuple-element.99, f32[16,4,128]{2,0,1:T(8,128)} %copy-done.34, f32[4,128,128]{2,1,0:T(8,128)} %fusion.148, ...), kind=kOutput, calls=%fused_computation.35 | convolution fusion | flops 410517504 | bytes 7782464 | tf_op jit(solution)/shard_map/transpose(jvp(hkts,kshp->kthp))/dot_general | solution.py:45
  292.2 2.6 copy.360
  294.9 2.3 reshape.339
  297.2 1.5 fusion.123
  298.7 3.4 fusion.55
  303.1 127.9 %reduce-scatter.2.cloned.1.call-done = f32[128,1024]{1,0:T(8,128)} async-done(((f32[4096,1024]{1,0:T(8,128)}), f32[128,1024]{1,0:T(8,128)}) %reduce-scatter.2.cloned.1.call-update) | async-done | bytes 524304 | tf_op jit(solution)/shard_map/reduce_scatter | solution.py:123
  (227 shorter events, 21.2 us)
Async XLA Ops:
  7.2 11.3 %copy-start = (bf16[512,128]{1,0:T(8,128)(2,1)S(1)}, bf16[512,128]{1,0:T(8,128)(2,1)}, u32[]{:S(2)}) copy-start(bf16[512,128]{1,0:T(8,128)(2,1)} %param.14) | copy-start | bytes 393220
  7.2 93.2 %all-gather.6.cloned.1.call-start = ((), (), s32[]{:S(2)}) async-start(), calls=%async_computation.7 | async-start | bytes 5242880 | tf_op jit(solution)/shard_map/all_gather | solution.py:81
  7.9 167.7 %all-gather.4.cloned.1.call-start = ((), (), s32[]{:S(2)}) async-start(), calls=%async_computation.5 | async-start | bytes 8650752 | tf_op jit(solution)/shard_map/all_gather | solution.py:80
  9.3 4.8 %copy-start.88 = (f32[16]{0:T(128)}, f32[16]{0:T(128)S(1)}, u32[]{:S(2)}) copy-start(f32[16]{0:T(128)S(1)} %exp.32) | copy-start | bytes 196
  12.3 3.8 copy-start.91
  14.2 4.2 copy-start.38
  16.0 2.5 copy-start.34
  16.8 3.2 copy-start.53
  16.8 3.2 copy-start.57
  16.8 3.2 copy-start.61
  17.3 2.7 copy-start.65
  17.3 2.7 copy-start.70
  17.3 2.7 copy-start.76
  23.0 26.5 %all-to-all-start = ((f32[1,16,32,3,128]{4,1,3,0,2:T(8,128)}), f32[1,16,32,3,128]{4,1,3,0,2:T(8,128)}, u32[]{:S(2)}, u32[]{:S(2)}) async-start(f32[1,16,32,3,128]{4,1,3,0,2:T(8,128)} %maximum_bitcast_fusion), calls=%async_computation | async-start | bytes 1572864 | tf_op jit(solution)/shard_map/all_to_all | solution.py:24
  63.8 17.4 %all-to-all-start.1 = ((f32[32,16,1,2,128]{4,3,1,2,0:T(2,128)}), f32[32,16,1,2,128]{4,3,1,2,0:T(2,128)}, u32[]{:S(2)}, u32[]{:S(2)}) async-start(f32[32,16,1,2,128]{4,3,1,2,0:T(2,128)} %copy.287), calls=%async_computation.1 | async-start | bytes 1048576 | tf_op jit(solution)/shard_map/all_to_all | solution.py:28
  68.5 362.4 %reduce-scatter.2.cloned.1.call-start = ((), (), s32[]{:S(2)}) async-start(), calls=%async_computation.6 | async-start | bytes 17301504 | tf_op jit(solution)/shard_map/reduce_scatter | solution.py:123
  175.6 12.4 %copy-start.6 = (f32[512,1024]{1,0:T(8,128)S(1)}, f32[512,1024]{1,0:T(8,128)}, u32[]{:S(2)}) copy-start(f32[512,1024]{1,0:T(8,128)} %reshape.341) | copy-start | bytes 6291460
  175.6 12.4 %copy-start.32 = (bf16[512,1024]{1,0:T(8,128)(2,1)S(1)}, bf16[512,1024]{1,0:T(8,128)(2,1)}, u32[]{:S(2)}) copy-start(bf16[512,1024]{1,0:T(8,128)(2,1)} %param.13) | copy-start | bytes 3145732
  175.6 12.4 %copy-start.85 = (f32[1024]{0:T(1024)S(1)}, f32[1024]{0:T(1024)}, u32[]{:S(2)}) copy-start(f32[1024]{0:T(1024)} %param.20) | copy-start | bytes 12292
  175.6 12.4 %copy-start.92 = (bf16[2048,1024]{1,0:T(8,128)(2,1)S(1)}, bf16[2048,1024]{1,0:T(8,128)(2,1)}, u32[]{:S(2)}) copy-start(bf16[2048,1024]{1,0:T(8,128)(2,1)} %all-gather.6.cloned.1.call-done) | copy-start | bytes 12582916
  188.0 9.0 %copy-start.84 = (f32[512]{0:T(512)}, f32[512]{0:T(512)S(1)}, u32[]{:S(2)}) copy-start(f32[512]{0:T(512)S(1)} %get-tuple-element.78) | copy-start | bytes 6148
  213.4 24.8 %all-to-all-start.2 = ((f32[1,16,32,2,128]{4,3,1,0,2:T(2,128)}), f32[1,16,32,2,128]{4,3,1,0,2:T(2,128)}, u32[]{:S(2)}, u32[]{:S(2)}) async-start(f32[1,16,32,2,128]{4,3,1,0,2:T(2,128)} %copy.303), calls=%async_computation.2 | async-start | bytes 1048576 | tf_op jit(solution)/shard_map/all_to_all | solution.py:24
  219.4 4.9 %copy-start.4 = (f32[4,128,16,64]{1,0,3,2:T(4,128)S(1)}, f32[4,128,16,64]{1,0,3,2:T(4,128)}, u32[]{:S(2)}) copy-start(f32[4,128,16,64]{1,0,3,2:T(4,128)} %reshape.325) | copy-start | bytes 6291460
  219.4 4.9 %copy-start.36 = (f32[16,4,128]{2,0,1:T(8,128)S(1)}, f32[16,4,128]{2,0,1:T(8,128)}, u32[]{:S(2)}) copy-start(f32[16,4,128]{2,0,1:T(8,128)} %copy-done.34) | copy-start | bytes 98308
  219.4 4.9 %copy-start.42 = (f32[4,128,128]{2,1,0:T(8,128)S(1)}, f32[4,128,128]{2,1,0:T(8,128)}, u32[]{:S(2)}) copy-start(f32[4,128,128]{2,1,0:T(8,128)} %fusion.148) | copy-start | bytes 786436
  219.4 4.9 %copy-start.49 = (f32[128,128]{1,0:T(8,128)S(1)}, f32[128,128]{1,0:T(8,128)}, u32[]{:S(2)}) copy-start(f32[128,128]{1,0:T(8,128)} %get-tuple-element.99) | copy-start | bytes 196612
  219.4 4.9 %copy-start.51 = (f32[16,4,128]{2,0,1:T(8,128)S(1)}, f32[16,4,128]{2,0,1:T(8,128)}, u32[]{:S(2)}) copy-start(f32[16,4,128]{2,0,1:T(8,128)} %get-tuple-element.94) | copy-start | bytes 98308
  219.5 4.9 %copy-start.75 = (pred[128,128]{1,0:T(8,128)(4,1)S(1)}, pred[128,128]{1,0:T(8,128)(4,1)}, u32[]{:S(2)}) copy-start(pred[128,128]{1,0:T(8,128)(4,1)} %get-tuple-element.98) | copy-start | bytes 49156
  240.2 6.3 %copy-start.33 = (f32[4,128,128]{2,1,0:T(8,128)S(1)}, f32[4,128,128]{2,1,0:T(8,128)}, u32[]{:S(2)}) copy-start(f32[4,128,128]{2,1,0:T(8,128)} %get-tuple-element.47) | copy-start | bytes 786436
  241.4 23.3 %all-to-all-start.3 = ((f32[32,16,1,2,128]{4,3,1,2,0:T(2,128)}), f32[32,16,1,2,128]{4,3,1,2,0:T(2,128)}, u32[]{:S(2)}, u32[]{:S(2)}) async-start(f32[32,16,1,2,128]{4,3,1,2,0:T(2,128)} %copy.306), calls=%async_computation.3 | async-start | bytes 1048576 | tf_op jit(solution)/shard_map/all_to_all | solution.py:28
  251.7 14.9 %copy-start.56 = (f32[16]{0:T(128)S(1)}, f32[16]{0:T(128)}, u32[]{:S(2)}) copy-start(f32[16]{0:T(128)} %copy-done.53) | copy-start | bytes 196
  251.7 14.9 %copy-start.60 = (f32[16]{0:T(128)S(1)}, f32[16]{0:T(128)}, u32[]{:S(2)}) copy-start(f32[16]{0:T(128)} %copy-done.57) | copy-start | bytes 196
  251.7 14.9 %copy-start.64 = (f32[16]{0:T(128)S(1)}, f32[16]{0:T(128)}, u32[]{:S(2)}) copy-start(f32[16]{0:T(128)} %copy-done.61) | copy-start | bytes 196
  251.7 15.0 %copy-start.68 = (f32[16]{0:T(128)S(1)}, f32[16]{0:T(128)}, u32[]{:S(2)}) copy-start(f32[16]{0:T(128)} %copy-done.65) | copy-start | bytes 196
  266.2 2.9 copy-start.11
  266.2 2.8 copy-start.13
  266.2 2.8 copy-start.15
  266.2 2.8 copy-start.17
  266.2 2.8 copy-start.19
  266.3 2.8 copy-start.21
  266.3 2.8 copy-start.69
  266.6 2.5 copy-start.9
  269.1 2.5 copy-start.47
  269.1 4.3 copy-start.3
  274.9 2.4 copy-start.28
  274.9 11.6 %copy-start.5 = (f32[4,128,16,64]{1,0,3,2:T(4,128)S(1)}, f32[4,128,16,64]{1,0,3,2:T(4,128)}, u32[]{:S(2)}) copy-start(f32[4,128,16,64]{1,0,3,2:T(4,128)} %reshape.325) | copy-start | bytes 6291460
  275.0 11.6 %copy-start.94 = (f32[16]{0:T(128)S(1)}, f32[16]{0:T(128)}, u32[]{:S(2)}) copy-start(f32[16]{0:T(128)} %param.19) | copy-start | bytes 196
  298.7 3.4 copy-start.27
  (54 other events, 98.5 us)
Sparse Core Ops, SparseCore 0:
  9.7 56.7 all-gather.5
  69.6 105.9 all-gather.3
  197.2 233.7 reduce-scatter.1
